TPU v7x, 32 devices: a whole 2x2x4 slice. The times are simulated.
32 devices in a mesh: row: 4 (over y, x), col: 8 (over z, core).
Axes of the slice: x: 2, y: 2, z: 4, core: 2. Of those that a mesh axis runs over, the one named last changes fastest.
Arguments:
- features: bfloat16 [32768, 128], P(('row', 'col')), may hold values from -6 to 6
- pair_index: int32 [2, 4096], P(None, ('row', 'col')), may hold values from -1 to 63, as said below
- bins: int32 [4096, 128, 128], P(('row', 'col')), may hold values from 0 to 8, as said below
- plate_weight: bfloat16 [1024, 128], replicated, may hold values from -0.1875 to 0.1875
- tower_weight: bfloat16 [1024, 128], replicated, may hold values from -0.1875 to 0.1875
- norm_gain: float32 [128], replicated, may hold values from 0.1 to 1.9
- update_in: bfloat16 [256, 128], replicated, may hold values from -0.375 to 0.375
- update_out: bfloat16 [128, 128], replicated, may hold values from -0.5 to 0.5
Outputs:
- updated: bfloat16 [32768, 128], P(('row', 'col'))
Inputs may be any that keep to these rules, and one draw needn't show every extreme that they name: `pair_index`: row 0 is a cluster of the meeting device's plate (below 64), row 1 a cluster of its tower (below 32). The 128 slots of one meeting device hold its live pairs first and then -1 in both rows. No cluster pair is live twice on one device. Some device has all 128 slots live. `bins`: 8 marks an atom pair that is no neighbour.
All inputs are finite; a program needn't handle non-finite values.
Results may differ from a plain program's by a relative error of at most 0.008.
Values may be sent and summed in bfloat16 or wider, within the bound.
A program may use at most 128 MiB of HBM per device.

v0:
```python
import jax
import jax.numpy as jnp
from jax import lax
from jax.sharding import PartitionSpec as P

D = 128
CLUSTER = 128
BINS = 8


def block_basis(pair_index, bins, turn, group):
    start = turn * group
    plate_idx = lax.dynamic_slice_in_dim(pair_index[0], start, group)
    tower_idx = lax.dynamic_slice_in_dim(pair_index[1], start, group)
    block = lax.dynamic_slice_in_dim(bins, start, group, 0)
    live = plate_idx >= 0
    levels = jnp.arange(BINS, dtype=jnp.int32)
    basis = (
        (block[:, :, None, :] == levels[None, None, :, None]) & live[:, None, None, None]
    ).astype(jnp.bfloat16)
    return (jnp.maximum(plate_idx, 0), jnp.maximum(tower_idx, 0), basis)


def plate_side(basis, tower, tower_at, plate_weight):
    count = basis.shape[0]
    near_plate = jnp.einsum(
        "gakb,gbd->gakd", basis, tower[tower_at], preferred_element_type=jnp.float32
    ).astype(jnp.bfloat16)
    message = jnp.dot(
        near_plate.reshape(count * CLUSTER, BINS * D),
        plate_weight,
        preferred_element_type=jnp.float32,
    )
    return message.reshape(count, CLUSTER, D)


def tower_side(basis, plate, plate_at, tower_weight):
    count = basis.shape[0]
    near_tower = jnp.einsum(
        "gakb,gad->gbkd", basis, plate[plate_at], preferred_element_type=jnp.float32
    ).astype(jnp.bfloat16)
    message = jnp.dot(
        near_tower.reshape(count * CLUSTER, BINS * D),
        tower_weight,
        preferred_element_type=jnp.float32,
    )
    return message.reshape(count, CLUSTER, D)


def return_tower(tower_acc, own_rows):
    flat = tower_acc.reshape(-1, D)
    summed = lax.psum(flat.astype(jnp.bfloat16), "row").astype(jnp.float32)
    return lax.dynamic_slice_in_dim(summed, lax.axis_index("row") * own_rows, own_rows, 0)


def return_plate(plate_acc, own_rows):
    flat = plate_acc.reshape(-1, D)
    summed = lax.psum(flat.astype(jnp.bfloat16), "col").astype(jnp.float32)
    return lax.dynamic_slice_in_dim(summed, lax.axis_index("col") * own_rows, own_rows, 0)


def shards(
    features, pair_index, bins, plate_weight, tower_weight, norm_gain, update_in, update_out
):
    own_rows = features.shape[0]
    plate = lax.all_gather(features, "col", axis=0, tiled=True).reshape(-1, CLUSTER, D)
    tower = lax.all_gather(features, "row", axis=0, tiled=True).reshape(-1, CLUSTER, D)
    group = 8
    slots = bins.shape[0]
    turns = slots // group
    plate_zero = jnp.zeros((plate.shape[0], CLUSTER, D), jnp.float32)
    tower_zero = jnp.zeros((tower.shape[0], CLUSTER, D), jnp.float32)

    def tower_step(turn, tower_acc):
        plate_at, tower_at, basis = block_basis(pair_index, bins, turn, group)
        return tower_acc.at[tower_at].add(tower_side(basis, plate, plate_at, tower_weight))

    def plate_step(turn, plate_acc):
        plate_at, tower_at, basis = block_basis(pair_index, bins, turn, group)
        return plate_acc.at[plate_at].add(plate_side(basis, tower, tower_at, plate_weight))

    tower_acc = lax.fori_loop(0, turns, tower_step, tower_zero)
    tower_back = return_tower(tower_acc, own_rows)
    plate_acc = lax.fori_loop(0, turns, plate_step, plate_zero)
    plate_back = return_plate(plate_acc, own_rows)
    incoming = plate_back + tower_back
    scale = lax.rsqrt(jnp.mean(incoming * incoming, axis=1, keepdims=True) + 1e-06)
    normed = (incoming * scale * norm_gain[None, :]).astype(jnp.bfloat16)
    joined = jnp.concatenate([features, normed], axis=1)
    hidden = jax.nn.silu(jnp.dot(joined, update_in, preferred_element_type=jnp.float32)).astype(
        jnp.bfloat16
    )
    result = features.astype(jnp.float32) + jnp.dot(
        hidden, update_out, preferred_element_type=jnp.float32
    )
    return result.astype(jnp.bfloat16)


def solution(mesh):
    placed = (
        P(("row", "col"), None),
        P(None, ("row", "col")),
        P(("row", "col"), None, None),
        P(),
        P(),
        P(),
        P(),
        P(),
    )
    return jax.shard_map(
        shards, mesh=mesh, in_specs=placed, out_specs=P(("row", "col"), None), check_vma=False
    )
```

profile of v0, /device:TPU:0, one launch (start us, length us, event | category | flops | bytes accessed | tf_op | source)
XLA Modules:
  0.0 342.1 jit_solution(12358343995069311886)
XLA Ops:
  8.1 30.4 %all-gather.3.cloned.1.call-done = bf16[4096,128]{1,0:T(8,128)(2,1)} async-done(((bf16[1024,128]{1,0:T(8,128)(2,1)}), bf16[4096,128]{1,0:T(8,128)(2,1)}) %all-gather.3.cloned.1.call-update) | async-done | bytes 1048592 | tf_op jit(solution)/shard_map/all_gather | solution.py:67
  38.4 2.5 broadcast_in_dim.38
  40.9 126.5 %while.26 = (s32[]{:T(128)}, f32[64,128,128]{2,1,0:T(8,128)}, s32[2,128]{1,0:T(2,128)S(1)}, s32[128,128,128]{2,1,0:T(8,128)}, bf16[32,128,128]{2,1,0:T(8,128)(2,...) while((s32[]{:T(128)}, f32[64,128,128]{2,1,0:T(8,128)}, ...), condition=%wide.region_2.0_spmd, body=%wide.region_0.0_spmd.sunk | while | flops 540148736 | bytes 8919471 | solution.py:84
  41.0 1.8 gather_fusion
  46.0 2.7 scatter_fusion
  48.9 1.8 gather_fusion
  51.9 1.3 fusion.67
  53.9 2.7 scatter_fusion
  56.7 1.8 gather_fusion
  59.7 1.3 fusion.67
  61.8 2.7 scatter_fusion
  64.6 1.8 gather_fusion
  67.6 1.3 fusion.67
  69.6 2.7 scatter_fusion
  72.4 1.8 gather_fusion
  75.4 1.3 fusion.67
  77.5 2.8 scatter_fusion
  80.3 1.8 gather_fusion
  83.3 1.3 fusion.67
  85.4 2.8 scatter_fusion
  88.2 1.8 gather_fusion
  91.2 1.3 fusion.67
  93.3 2.8 scatter_fusion
  96.2 1.8 gather_fusion
  99.2 1.3 fusion.67
  101.2 2.8 scatter_fusion
  104.1 1.8 gather_fusion
  107.1 1.3 fusion.67
  109.1 2.8 scatter_fusion
  112.0 1.8 gather_fusion
  115.0 1.3 fusion.67
  117.1 2.8 scatter_fusion
  119.9 1.8 gather_fusion
  122.9 1.3 fusion.67
  125.0 2.8 scatter_fusion
  127.9 1.8 gather_fusion
  132.9 2.8 scatter_fusion
  135.8 1.8 gather_fusion
  140.8 2.8 scatter_fusion
  143.7 1.8 gather_fusion
  148.8 2.8 scatter_fusion
  151.6 1.8 gather_fusion
  156.7 2.8 scatter_fusion
  159.6 1.8 gather_fusion
  164.6 2.8 scatter_fusion
  167.4 3.9 %convert_element_type.54 = bf16[64,128,128]{2,1,0:T(8,128)(2,1)} convert(f32[64,128,128]{2,1,0:T(8,128)} %get-tuple-element.223) | non-fusion elementwise | flops 1048576 | bytes 6291456 | tf_op jit(solution)/shard_map/convert_element_type | solution.py:58
  172.3 105.5 %while.27 = (s32[]{:T(128)}, f32[32,128,128]{2,1,0:T(8,128)S(1)}, s32[2,128]{1,0:T(2,128)S(1)}, bf16[64,128,128]{2,1,0:T(8,128)(2,1)}, s32[128,128,128]{2,1,0:T(...) while((s32[]{:T(128)}, f32[32,128,128]{2,1,0:T(8,128)S(1)}, ...), condition=%wide.region_6.0_spmd, body=%wide.region_4.0_spmd.sunk | while | flops 540148736 | bytes 8919471 | solution.py:82
  172.4 2.2 gather_fusion.1
  178.9 2.2 gather_fusion.1
  185.5 2.2 gather_fusion.1
  192.2 2.2 gather_fusion.1
  198.8 2.2 gather_fusion.1
  205.4 2.2 gather_fusion.1
  211.9 2.2 gather_fusion.1
  218.6 2.2 gather_fusion.1
  225.2 2.2 gather_fusion.1
  231.7 2.2 gather_fusion.1
  238.3 2.2 gather_fusion.1
  244.9 2.2 gather_fusion.1
  251.5 2.2 gather_fusion.1
  258.1 2.2 gather_fusion.1
  264.7 2.2 gather_fusion.1
  271.3 2.2 gather_fusion.1
  279.0 52.8 %all-reduce.5.cloned.1.call-done = bf16[4096,128]{1,0:T(8,128)(2,1)} async-done(((bf16[4096,128]{1,0:T(8,128)(2,1)}), bf16[4096,128]{1,0:T(8,128)(2,1)}) %all-reduce.5.cloned.1.call-update) | async-done | bytes 1048592 | tf_op jit(solution)/shard_map/psum | solution.py:52
  (260 shorter events, 116.4 us)
Async XLA Ops:
  6.5 327.7 %copy-start = (bf16[256,128]{1,0:T(8,128)(2,1)S(1)}, bf16[256,128]{1,0:T(8,128)(2,1)}, u32[]{:S(2)}) copy-start(bf16[256,128]{1,0:T(8,128)(2,1)} %param.18) | copy-start | bytes 196612
  6.5 31.9 %all-gather.3.cloned.1.call-start = ((), (), s32[]{:S(2)}) async-start(), calls=%async_computation | async-start | bytes 1310720 | tf_op jit(solution)/shard_map/all_gather | solution.py:67
  7.3 164.1 %all-gather.5.cloned.1.call-start = ((), (), s32[]{:S(2)}) async-start(), calls=%async_computation.2 | async-start | bytes 2359296 | tf_op jit(solution)/shard_map/all_gather | solution.py:66
  8.0 271.0 %all-reduce.3.cloned.1.call-start = ((), (), s32[]{:S(2)}) async-start(), calls=%async_computation.1 | async-start | bytes 4194304 | tf_op jit(solution)/shard_map/psum | solution.py:58
  38.4 2.5 copy-start.1
  38.4 2.5 copy-start.4
  171.3 0.9 copy-start.2
  171.3 160.4 %all-reduce.5.cloned.1.call-start = ((), (), s32[]{:S(2)}) async-start(), calls=%async_computation.3 | async-start | bytes 2097152 | tf_op jit(solution)/shard_map/psum | solution.py:52
  277.7 55.3 %copy-start.5 = (f32[128]{0:T(128)S(1)}, f32[128]{0:T(128)}, u32[]{:S(2)}) copy-start(f32[128]{0:T(128)} %param.17) | copy-start | bytes 1540
  277.8 56.5 %copy-start.3 = (bf16[1024,128]{1,0:T(8,128)(2,1)S(1)}, bf16[1024,128]{1,0:T(8,128)(2,1)}, u32[]{:S(2)}) copy-start(bf16[1024,128]{1,0:T(8,128)(2,1)} %param.12) | copy-start | bytes 786436
  277.8 56.5 %copy-start.6 = (bf16[128,128]{1,0:T(8,128)(2,1)S(1)}, bf16[128,128]{1,0:T(8,128)(2,1)}, u32[]{:S(2)}) copy-start(bf16[128,128]{1,0:T(8,128)(2,1)} %param.19) | copy-start | bytes 98308
Sparse Core Ops, SparseCore 0:
  9.2 29.2 all-gather.2
  40.0 29.1 all-gather.4
  171.5 65.3 all-reduce.2
  279.1 52.6 all-reduce.4
where the time goes:
time: 346 us; the launch traced here: 342 us
  local copies, waits for them, and re-layouts  102 us (29%)
  waiting for transfers between devices  84.6 us (24%)
  other arithmetic  73.4 us (21%)
  matrix products  67 us (19%)
  between operations  13.2 us (4%)
    psum x1, waiting for transfers between devices, return_tower(): summed = lax.psum(flat.astype(jnp.bfloat16), 'row').astype(jnp.float32)  52.8 us
    scatter-add x16, other arithmetic, plate_step(): plate_acc.at[plate_at].add(plate_side(basis, tower, tower_at, plate_weight))  44.1 us
    gather x16, local copies, waits for them, and re-layouts, tower_side(): plate[plate_at]  35.2 us
    dynamic_slice x32, local copies, waits for them, and re-layouts, block_basis(): block = lax.dynamic_slice_in_dim(bins, start, group, 0)  34.5 us
    all_gather x1, waiting for transfers between devices, shards(): lax.all_gather(features, 'row', axis=0, tiled=True).reshape(-1, CLUSTER, D)  30.4 us
    gather x16, local copies, waits for them, and re-layouts, plate_side(): tower[tower_at]  29.2 us
    dot_general x16, matrix products, plate_side(): jnp.einsum('gakb,gbd->gakd', basis, tower[tower_at], preferred_element_ty...  20.9 us
    dot_general x16, matrix products, tower_side(): jnp.einsum('gakb,gad->gbkd', basis, plate[plate_at], preferred_element_ty...  20.8 us
  transfers between devices with their start and end apart: 4, of which 2 were waited for; matrix products, arithmetic and copies ran while one was open for 70% of the time, Pallas kernels for 0%

commit v1 on v0

v1 whole, which is shorter than its diff:
```python
import functools

import jax
import jax.numpy as jnp
from jax import lax
from jax.experimental import pallas as pl
from jax.experimental.pallas import tpu as pltpu
from jax.sharding import PartitionSpec as P

D = 128
CLUSTER = 128
BINS = 8
GROUP = 8


def side_kernel(transposed, own_row, idx_ref, far_ref, weight_ref, bins_ref, out_ref, table, acc):
    step = pl.program_id(0)

    @pl.when(step == 0)
    def _():
        acc[...] = jnp.zeros_like(acc)

        @pl.loop(0, table.shape[0])
        def _(c):
            rows = far_ref[pl.ds(pl.multiple_of(c * CLUSTER, CLUSTER), CLUSTER), :]
            mapped = jnp.dot(rows, weight_ref[...], preferred_element_type=jnp.float32)
            for k in range(BINS):
                table[c, k * CLUSTER:(k + 1) * CLUSTER, :] = mapped[:, k * D:(k + 1) * D].astype(jnp.bfloat16)

    @pl.when(idx_ref[0, step * GROUP] >= 0)
    def _():
        for g in range(GROUP):
            own = idx_ref[own_row, step * GROUP + g]
            far = idx_ref[1 - own_row, step * GROUP + g]
            live = own >= 0
            block = jnp.where(live, bins_ref[g], BINS).astype(jnp.float32)
            if transposed:
                block = block.T
            block = block.astype(jnp.bfloat16)
            one = jnp.ones_like(block)
            zero = jnp.zeros_like(block)
            basis = jnp.concatenate(
                [jnp.where(block == jnp.bfloat16(k), one, zero) for k in range(BINS)], axis=1
            )
            own = jnp.maximum(own, 0)
            far = jnp.maximum(far, 0)
            acc[own] += jnp.dot(basis, table[far], preferred_element_type=jnp.float32)

    @pl.when(step == pl.num_programs(0) - 1)
    def _():
        out_ref[...] = acc[...].astype(jnp.bfloat16)


def side(pair_index, far, weight, bins, own_clusters, own_row):
    slots = bins.shape[0]
    far_clusters = far.shape[0] // CLUSTER
    whole = lambda *_: (0, 0)
    wide = weight.reshape(BINS, D, D).transpose(1, 0, 2).reshape(D, BINS * D)
    return pl.pallas_call(
        functools.partial(side_kernel, own_row == 1, own_row),
        grid_spec=pltpu.PrefetchScalarGridSpec(
            num_scalar_prefetch=1,
            grid=(slots // GROUP,),
            in_specs=[
                pl.BlockSpec(far.shape, whole, pipeline_mode=pl.Buffered(1)),
                pl.BlockSpec(wide.shape, whole, pipeline_mode=pl.Buffered(1)),
                pl.BlockSpec((GROUP, CLUSTER, CLUSTER), lambda s, _: (s, 0, 0)),
            ],
            out_specs=pl.BlockSpec(
                (own_clusters, CLUSTER, D), lambda *_: (0, 0, 0), pipeline_mode=pl.Buffered(1)
            ),
            scratch_shapes=[
                pltpu.VMEM((far_clusters, BINS * CLUSTER, D), jnp.bfloat16),
                pltpu.VMEM((own_clusters, CLUSTER, D), jnp.float32),
            ],
        ),
        out_shape=jax.ShapeDtypeStruct((own_clusters, CLUSTER, D), jnp.bfloat16),
        compiler_params=pltpu.CompilerParams(vmem_limit_bytes=60 * 1024 * 1024),
    )(pair_index, far, wide, bins)


def shards(
    features, pair_index, bins, plate_weight, tower_weight, norm_gain, update_in, update_out
):
    tower = lax.all_gather(features, "row", axis=0, tiled=True)
    plate = lax.all_gather(features, "col", axis=0, tiled=True)
    plates = plate.shape[0] // CLUSTER
    towers = tower.shape[0] // CLUSTER
    plate_part = side(pair_index, tower, plate_weight, bins, plates, 0)
    tower_part = side(pair_index, plate, tower_weight, bins, towers, 1)
    plate_back = lax.psum_scatter(plate_part.reshape(-1, D), "col", scatter_dimension=0, tiled=True)
    tower_back = lax.psum_scatter(tower_part.reshape(-1, D), "row", scatter_dimension=0, tiled=True)
    incoming = plate_back.astype(jnp.float32) + tower_back.astype(jnp.float32)
    scale = lax.rsqrt(jnp.mean(incoming * incoming, axis=1, keepdims=True) + 1e-06)
    normed = (incoming * scale * norm_gain[None, :]).astype(jnp.bfloat16)
    joined = jnp.concatenate([features, normed], axis=1)
    hidden = jax.nn.silu(jnp.dot(joined, update_in, preferred_element_type=jnp.float32)).astype(
        jnp.bfloat16
    )
    result = features.astype(jnp.float32) + jnp.dot(
        hidden, update_out, preferred_element_type=jnp.float32
    )
    return result.astype(jnp.bfloat16)


def solution(mesh):
    placed = (
        P(("row", "col"), None),
        P(None, ("row", "col")),
        P(("row", "col"), None, None),
        P(),
        P(),
        P(),
        P(),
        P(),
    )
    return jax.shard_map(
        shards, mesh=mesh, in_specs=placed, out_specs=P(("row", "col"), None), check_vma=False
    )
```

time: 346 us -> 147 us (0.42)
  local copies, waits for them, and re-layouts: 102 us -> 3.69 us
  other arithmetic: 73.4 us -> 2.48 us
  matrix products: 67 us -> 1.24 us
  Pallas kernels: 0 us -> 46.8 us
  waiting for transfers between devices: 84.6 us -> 78.9 us
    dot_general x64 -> x0, matrix products: 65.8 us -> none  [the longest x16 20.9 us: plate_side(): jnp.einsum('gakb,gbd->gakd', basis, tower[tower_at], preferred_element_ty...]
    gather x32 -> x0, local copies, waits for them, and re-layouts: 64.3 us -> none  [the longest x16 35.2 us: tower_side(): plate[plate_at]]
    scatter-add x32 -> x0, other arithmetic: 60.6 us -> none  [the longest x16 44.1 us: plate_step(): plate_acc.at[plate_at].add(plate_side(basis, tower, tower_at, plate_weight))]
    psum x2 -> x0, waiting for transfers between devices: 52.8 us -> none  [the longest x1 52.8 us: return_tower(): summed = lax.psum(flat.astype(jnp.bfloat16), 'row').astype(jnp.float32)]
    pallas_call x0 -> x2, Pallas kernels: none -> 46.8 us  [side(): pl.pallas_call(functools.partial(side_kernel, own_row == 1, own_row), gri...]
    reduce_scatter x0 -> x2, waiting for transfers between devices: none -> 40 us  [the longest x1 29.1 us: shards(): lax.psum_scatter(tower_part.reshape(-1, D), 'row', scatter_dimension=0, t...]
    dynamic_slice x32 -> x0, local copies, waits for them, and re-layouts: 34.5 us -> none  [block_basis(): block = lax.dynamic_slice_in_dim(bins, start, group, 0)]
    all_gather x2, waiting for transfers between devices: 30.4 us -> 37.4 us  [the longest x1 28.5 us: shards(): tower = lax.all_gather(features, 'row', axis=0, tiled=True)]
  transfers between devices with their start and end apart: 4 -> 4, of which waited for: 2 -> 4; matrix products, arithmetic and copies ran while one was open for 70% -> 2% of each run, Pallas kernels for 0% -> 32%
where the time goes in v1:
time: 147 us; the launch traced here: 146 us
  waiting for transfers between devices  78.9 us (54%)
  Pallas kernels  46.8 us (32%)
  between operations  13.2 us (9%)
  local copies, waits for them, and re-layouts  3.69 us (3%)
  other arithmetic  2.48 us (2%)
    pallas_call x2, Pallas kernels, side(): pl.pallas_call(functools.partial(side_kernel, own_row == 1, own_row), gri...  46.8 us
    reduce_scatter x1, waiting for transfers between devices, shards(): lax.psum_scatter(tower_part.reshape(-1, D), 'row', scatter_dimension=0, t...  29.1 us
    all_gather x1, waiting for transfers between devices, shards(): tower = lax.all_gather(features, 'row', axis=0, tiled=True)  28.5 us
    reduce_scatter x1, waiting for transfers between devices, shards(): lax.psum_scatter(plate_part.reshape(-1, D), 'col', scatter_dimension=0, t...  10.9 us
    all_gather x1, waiting for transfers between devices, shards(): plate = lax.all_gather(features, 'col', axis=0, tiled=True)  8.93 us
  transfers between devices with their start and end apart: 4, of which 4 were waited for; matrix products, arithmetic and copies ran while one was open for 2% of the time, Pallas kernels for 32%

profile of v1, /device:TPU:0, one launch (start us, length us, event | category | flops | bytes accessed | tf_op | source)
XLA Modules:
  0.0 146.4 jit_solution(18251985713968229091)
XLA Ops:
  6.5 0.0 copy-start
  6.5 0.0 all-gather.3.cloned.1.call-start
  6.5 0.7 all-gather.3.cloned.1.call-update
  7.3 0.0 all-gather.5.cloned.1.call-start
  7.3 0.7 all-gather.5.cloned.1.call-update
  8.0 0.0 reduce-scatter.3.cloned.1.call-start
  8.1 1.1 copy.9
  9.2 0.8 copy.16
  9.9 28.5 %all-gather.3.cloned.1.call-done.far_ref = bf16[4096,128]{1,0:T(8,128)(2,1)} async-done(((bf16[1024,128]{1,0:T(8,128)(2,1)}), bf16[4096,128]{1,0:T(8,128)(2,1)}) %all-gather.3.cloned.1.call-update) | async-done | bytes 1048592 | tf_op jit(solution)/shard_map/all_gather | solution.py:85
  38.4 20.0 %shard_map.82 = bf16[64,128,128]{2,1,0:T(8,128)(2,1)} custom-call(s32[2,128]{1,0:T(2,128)} %idx_ref.3, bf16[4096,128]{1,0:T(8,128)(2,1)} %all-gather.3.cloned.1.call-done.far_ref, bf16[128,1024]{1,0:T(8,128)(2,1)} %bitcast.18, s32[128,128,128]{2,1,0:T(8,128)} %bins_ref.3), custom_call_target="tpu_custom_call" | custom-call | tf_op jit(solution)/shard_map/pallas_call | solution.py:59
  58.4 0.0 copy-start.2
  58.4 0.0 reduce-scatter.3.cloned.1.call-update
  58.4 0.0 reduce-scatter.5.cloned.1.call-start
  58.5 0.9 copy-done.2
  59.3 0.2 copy.10
  59.5 0.8 copy.15
  60.3 8.9 %all-gather.5.cloned.1.call-done.far_ref = bf16[8192,128]{1,0:T(8,128)(2,1)} async-done(((bf16[1024,128]{1,0:T(8,128)(2,1)}), bf16[8192,128]{1,0:T(8,128)(2,1)}) %all-gather.5.cloned.1.call-update) | async-done | bytes 2097168 | tf_op jit(solution)/shard_map/all_gather | solution.py:86
  69.2 0.0 copy-start.3
  69.2 26.9 %shard_map.83 = bf16[32,128,128]{2,1,0:T(8,128)(2,1)} custom-call(s32[2,128]{1,0:T(2,128)} %idx_ref.3, bf16[8192,128]{1,0:T(8,128)(2,1)} %all-gather.5.cloned.1.call-done.far_ref, bf16[128,1024]{1,0:T(8,128)(2,1)} %bitcast.19, s32[128,128,128]{2,1,0:T(8,128)} %bins_ref.3), custom_call_target="tpu_custom_call" | custom-call | tf_op jit(solution)/shard_map/pallas_call | solution.py:59
  96.1 0.0 copy-start.1
  96.1 0.0 copy-start.4
  96.1 0.0 reduce-scatter.5.cloned.1.call-update
  96.1 10.9 %reduce-scatter.3.cloned.1.call-done = bf16[1024,128]{1,0:T(8,128)(2,1)} async-done(((bf16[8192,128]{1,0:T(8,128)(2,1)}), bf16[1024,128]{1,0:T(8,128)(2,1)}) %reduce-scatter.3.cloned.1.call-update) | async-done | bytes 262160 | tf_op jit(solution)/shard_map/reduce_scatter | solution.py:91
  107.0 29.1 %reduce-scatter.5.cloned.1.call-done = bf16[1024,128]{1,0:T(8,128)(2,1)} async-done(((bf16[4096,128]{1,0:T(8,128)(2,1)}), bf16[1024,128]{1,0:T(8,128)(2,1)}) %reduce-scatter.5.cloned.1.call-update) | async-done | bytes 262160 | tf_op jit(solution)/shard_map/reduce_scatter | solution.py:92
  136.1 1.2 multiply_reduce_fusion
  137.4 0.0 copy-done.3
  137.4 1.2 multiply_convert_fusion.1
  138.6 0.0 copy-done
  138.6 0.0 copy-done.1
  138.6 0.0 copy-done.4
  138.7 1.2 fusion
  (1 shorter events, 0.0 us)
Async XLA Ops:
  6.5 132.1 %copy-start = (bf16[256,128]{1,0:T(8,128)(2,1)S(1)}, bf16[256,128]{1,0:T(8,128)(2,1)}, u32[]{:S(2)}) copy-start(bf16[256,128]{1,0:T(8,128)(2,1)} %param.14) | copy-start | bytes 196612
  6.5 31.9 %all-gather.3.cloned.1.call-start = ((), (), s32[]{:S(2)}) async-start(), calls=%async_computation.2 | async-start | bytes 1310720 | tf_op jit(solution)/shard_map/all_gather | solution.py:85
  7.3 61.9 %all-gather.5.cloned.1.call-start = ((), (), s32[]{:S(2)}) async-start(), calls=%async_computation.4 | async-start | bytes 2359296 | tf_op jit(solution)/shard_map/all_gather | solution.py:86
  8.0 99.0 %reduce-scatter.3.cloned.1.call-start = ((), (), s32[]{:S(2)}) async-start(), calls=%async_computation.3 | async-start | bytes 2359296 | tf_op jit(solution)/shard_map/reduce_scatter | solution.py:91
  58.4 0.9 copy-start.2
  58.4 77.7 %reduce-scatter.5.cloned.1.call-start = ((), (), s32[]{:S(2)}) async-start(), calls=%async_computation.5 | async-start | bytes 1310720 | tf_op jit(solution)/shard_map/reduce_scatter | solution.py:92
  69.2 68.2 %copy-start.3 = (f32[128]{0:T(128)S(1)}, f32[128]{0:T(128)}, u32[]{:S(2)}) copy-start(f32[128]{0:T(128)} %param.13) | copy-start | bytes 1540
  96.1 42.6 %copy-start.1 = (bf16[1024,128]{1,0:T(8,128)(2,1)S(1)}, bf16[1024,128]{1,0:T(8,128)(2,1)}, u32[]{:S(2)}) copy-start(bf16[1024,128]{1,0:T(8,128)(2,1)} %param.8) | copy-start | bytes 786436
  96.1 42.6 %copy-start.4 = (bf16[128,128]{1,0:T(8,128)(2,1)S(1)}, bf16[128,128]{1,0:T(8,128)(2,1)}, u32[]{:S(2)}) copy-start(bf16[128,128]{1,0:T(8,128)(2,1)} %param.15) | copy-start | bytes 98308
Sparse Core Ops, SparseCore 0:
  9.2 29.2 all-gather.2
  40.0 29.1 all-gather.4
  71.5 35.4 reduce-scatter.2
  109.8 26.3 reduce-scatter.4
